TPU v7x, 512 devices: a whole 4x8x8 slice. The times are simulated.
512 devices in a mesh: ctx: 16 (over z, core), tis: 8 (over y), rep: 4 (over x).
Axes of the slice: x: 4, y: 8, z: 8, core: 2. Of those that a mesh axis runs over, the one named last changes fastest.
Arguments:
- donor_feat: bfloat16 [4, 256, 256], P('rep', 'ctx'), may hold values from -6 to 6
- acceptor_feat: bfloat16 [4, 256, 256], P('rep', 'ctx'), may hold values from -6 to 6
- donor_pos: int32 [4, 256], P('rep', 'ctx'), may hold values from 0 to 65535
- acceptor_pos: int32 [4, 256], P('rep'), may hold values from 0 to 65535
- pair_mask: int32 [4, 256, 80], P('rep', 'ctx'), may hold values from 0 to 1
- targets: int32 [4, 256, 32], P('rep', 'ctx', 'tis'), may hold values from 0 to 80, as said below
- dist_table: bfloat16 [128, 256], replicated, may hold values from -3 to 3
- hidden_weights: bfloat16 [32, 256, 512], P('tis'), may hold values from -0.375 to 0.375
- output_weights: bfloat16 [32, 512], P('tis')
Outputs:
- donor_loss: float32 [4, 256, 32], P('rep', 'ctx', 'tis')
- grad_hidden: float32 [32, 256, 512], P('tis', ('ctx', 'rep'))
- grad_acceptor: float32 [4, 256, 256], P('rep', 'ctx')
Inputs may be any that keep to these rules, and one draw needn't show every extreme that they name: `targets`: each target is a valid slot of its donor, or 80 for no splice.
All inputs are finite; a program needn't handle non-finite values.
Results may differ from a plain program's by a relative error of at most 0.002.
The roundings to bfloat16 on the way count: a program that leaves them out, or rounds other values in their place, can miss the bound.
Values may be sent and summed in bfloat16 or wider, within the bound.
A program may use at most 64 MiB of HBM per device.

v0:
```python
import jax
import jax.numpy as jnp
from jax import lax
from jax.sharding import PartitionSpec as P

BLOCK_BP = 65536
SPAN_BLOCKS = 4
BIN_BP = 2048
BINS = 128


def passed_along(value, axis, steps):
    count = lax.axis_size(axis)
    first, last = (max(0, -steps), min(count, count - steps))
    return lax.ppermute(value, axis, [(source, source + steps) for source in range(first, last)])


def silu_grad(values):
    sig = jax.nn.sigmoid(values)
    return sig * (1.0 + values * (1.0 - sig))


def on_device(
    donor_feat,
    acceptor_feat,
    donor_pos,
    acceptor_pos,
    pair_mask,
    targets,
    dist_table,
    hidden_weights,
    output_weights,
):
    seq_dev, don_blk, width = donor_feat.shape
    acc_blk = acceptor_feat.shape[1]
    blocks = lax.axis_size("ctx")
    reach = SPAN_BLOCKS + 1
    slots = reach * acc_blk
    here = lax.axis_index("ctx")
    pieces = [acceptor_feat]
    current = acceptor_feat
    for offset in range(1, reach):
        current = passed_along(current, "ctx", -1)
        pieces.append(current)
    window = jnp.stack(pieces, axis=1).reshape(seq_dev, slots, width)
    pos_pad = jnp.concatenate(
        [acceptor_pos, jnp.zeros((seq_dev, SPAN_BLOCKS * acc_blk), jnp.int32)], axis=1
    )
    pos_win = lax.dynamic_slice_in_dim(pos_pad, here * acc_blk, slots, 1)
    slot_block = jnp.arange(slots, dtype=jnp.int32) // acc_blk
    inchain = here + slot_block < blocks
    dist = slot_block * BLOCK_BP + pos_win[:, None, :] - donor_pos[:, :, None]
    valid = (pair_mask > 0) & (dist > 0) & (dist <= SPAN_BLOCKS * BLOCK_BP) & inchain[None, None, :]
    bins = jnp.clip((dist - 1) // BIN_BP, 0, BINS - 1)
    lookup = (
        (bins[..., None] == jnp.arange(BINS, dtype=jnp.int32))
        .astype(jnp.bfloat16)
        .reshape(-1, BINS)
    )
    table = jnp.dot(lookup, dist_table, preferred_element_type=jnp.float32).reshape(
        seq_dev, don_blk, slots, width
    )
    pre = (
        donor_feat.astype(jnp.float32)[:, :, None, :] + window.astype(jnp.float32)[:, None] + table
    )
    flat = jax.nn.silu(pre).astype(jnp.bfloat16).reshape(-1, width)
    grad_pair = jnp.zeros((flat.shape[0], width), jnp.float32)
    losses = []
    fulls = []
    slot_ids = jnp.arange(slots, dtype=jnp.int32)
    for tissue in range(hidden_weights.shape[0]):
        w_in = hidden_weights[tissue]
        w_out = output_weights[tissue]
        goal = targets[:, :, tissue]
        hid = jnp.dot(flat, w_in, preferred_element_type=jnp.float32)
        act = jax.nn.silu(hid).astype(jnp.bfloat16)
        logits = jnp.dot(act, w_out, preferred_element_type=jnp.float32).reshape(
            seq_dev, don_blk, slots
        )
        masked = jnp.where(valid, logits, -jnp.inf)
        top = jnp.maximum(jnp.max(masked, axis=-1), 0.0)
        expo = jnp.exp(masked - top[..., None])
        total = jnp.sum(expo, axis=-1) + jnp.exp(-top)
        picked = jnp.take_along_axis(logits, jnp.minimum(goal, slots - 1)[..., None], axis=-1)[
            ..., 0
        ]
        picked = jnp.where(goal == slots, 0.0, picked)
        losses.append(top + jnp.log(total) - picked)
        onehot = (goal[..., None] == slot_ids).astype(jnp.float32)
        grad_logits = expo / total[..., None] - onehot
        grad_act = grad_logits.reshape(-1)[:, None] * w_out.astype(jnp.float32)[None, :]
        grad_hid = (grad_act * silu_grad(hid)).astype(jnp.bfloat16)
        grad_pair = grad_pair + lax.dot_general(
            grad_hid, w_in, (((1,), (1,)), ((), ())), preferred_element_type=jnp.float32
        )
        fulls.append(
            lax.dot_general(
                flat, grad_hid, (((0,), (0,)), ((), ())), preferred_element_type=jnp.float32
            )
        )
    stacked = jnp.stack(fulls, axis=1)
    grad_hidden = jnp.transpose(
        lax.psum_scatter(stacked, ("ctx", "rep"), scatter_dimension=0, tiled=True), (1, 0, 2)
    )
    grad_pre = grad_pair.reshape(seq_dev, don_blk, slots, width) * silu_grad(pre)
    contrib = jnp.sum(grad_pre, axis=1).reshape(seq_dev, reach, acc_blk, width)
    carried = contrib[:, reach - 1]
    for offset in range(reach - 2, -1, -1):
        carried = passed_along(carried, "ctx", 1) + contrib[:, offset]
    grad_acceptor = lax.psum(carried, "tis")
    donor_loss = jnp.stack(losses, axis=-1)
    return (donor_loss, grad_hidden, grad_acceptor)


def solution(mesh):
    placed = (
        P("rep", "ctx", None),
        P("rep", "ctx", None),
        P("rep", "ctx"),
        P("rep", None),
        P("rep", "ctx", None),
        P("rep", "ctx", "tis"),
        P(),
        P("tis", None, None),
        P("tis", None),
    )
    return jax.shard_map(
        on_device,
        mesh=mesh,
        in_specs=placed,
        out_specs=(P("rep", "ctx", "tis"), P("tis", ("ctx", "rep"), None), P("rep", "ctx", None)),
        check_vma=False,
    )
```

profile of v0, /device:TPU:8, one launch (start us, length us, event | category | flops | bytes accessed | tf_op | source)
XLA Modules:
  0.0 280.9 jit_solution(4810384354852864490)
XLA Ops:
  7.2 1.3 collective-permute-start
  8.5 0.7 constant_dynamic-update-slice_fusion.4
  9.2 0.7 bitcast_convert_fusion.1
  9.9 0.8 slice_bitcast_fusion.8
  10.8 0.9 slice_reduce_fusion.3
  11.6 0.8 bitcast_add_fusion.4
  12.4 0.7 fusion.28
  13.2 1.3 collective-permute-start.1
  14.6 2.4 collective-permute-done.1
  16.9 1.3 collective-permute-start.2
  18.2 3.9 %collective-permute-done.2 = bf16[1,16,256]{2,1,0:T(8,128)(2,1)S(1)} collective-permute-done((bf16[1,16,256]{2,1,0:T(8,128)(2,1)S(1)}, bf16[1,16,256]{2,1,0:T(8,128)(2,1)S(1)}, u32[]{:S(2)}, u32[]{:S(2)}) %collective-permute-start.2) | collective-permute-done | bytes 8224 | tf_op jit(solution)/shard_map/ppermute | solution.py:15
  22.2 1.3 collective-permute-start.3
  23.5 3.7 %collective-permute-done.3 = bf16[1,16,256]{2,1,0:T(8,128)(2,1)S(1)} collective-permute-done((bf16[1,16,256]{2,1,0:T(8,128)(2,1)S(1)}, bf16[1,16,256]{2,1,0:T(8,128)(2,1)S(1)}, u32[]{:S(2)}, u32[]{:S(2)}) %collective-permute-start.3) | collective-permute-done | bytes 8224 | tf_op jit(solution)/shard_map/ppermute | solution.py:15
  27.2 1.7 multiply_convert_fusion.8
  28.9 0.9 multiply_convert_fusion.7
  29.7 2.3 multiply_convert_fusion.4
  32.0 2.3 multiply_convert_fusion.5
  34.3 2.3 multiply_convert_fusion.6
  37.2 0.6 fusion.42
  37.7 0.6 fusion.44
  38.3 0.6 fusion.46
  39.5 1.0 multiply_convert_fusion.3
  40.5 1.4 convolution_bitcast_fusion.3
  41.9 2.5 fusion.10
  44.5 2.7 multiply_convert_fusion
  47.2 1.3 convolution_bitcast_fusion
  48.6 2.7 multiply_convert_fusion.1
  51.3 1.3 convolution_bitcast_fusion.1
  52.8 2.7 multiply_convert_fusion.2
  56.0 0.8 copy-done.1
  57.1 0.6 convolution_add_fusion.2
  57.7 0.6 convolution_add_fusion.1
  58.9 0.7 copy-done.5
  60.1 4.3 %collective-permute-start.4 = (f32[1,16,256]{2,1,0:T(8,128)S(1)}, f32[1,16,256]{2,1,0:T(8,128)S(1)}, u32[]{:S(2)}, u32[]{:S(2)}) collective-permute-start(f32[1,16,256]{2,1,0:T(8,128)S(1)} %slice_bitcast_fusion.4), channel_id=1, source_target_pairs={{0,32},{32,64},{64,96},{96,128},{128,160},{160,192},{192,224},{224... | collective-permute-start | bytes 49160 | tf_op jit(solution)/shard_map/ppermute | solution.py:15
  64.5 1.5 pad_maximum_fusion
  66.0 2.0 collective-permute-start.5
  68.0 1.3 dynamic-slice
  70.0 0.7 gather_fusion
  70.6 0.7 gather_fusion.1
  71.3 0.7 gather_fusion.3
  72.0 0.7 gather_fusion.2
  72.6 4.3 %collective-permute-start.6 = (f32[1,16,256]{2,1,0:T(8,128)S(1)}, f32[1,16,256]{2,1,0:T(8,128)S(1)}, u32[]{:S(2)}, u32[]{:S(2)}) collective-permute-start(f32[1,16,256]{2,1,0:T(8,128)S(1)} %fusion.25), channel_id=1, source_target_pairs={{0,32},{32,64},{64,96},{96,128},{128,160},{160,192},{192,224},{224... | collective-permute-start | bytes 49160 | tf_op jit(solution)/shard_map/ppermute | solution.py:15
  77.0 0.8 collective-permute-done.6
  77.8 2.2 collective-permute-start.7
  80.0 0.6 pad_maximum_fusion.1
  80.8 30.4 %psum.7 = f32[1,16,256]{2,1,0:T(8,128)} all-reduce(f32[1,16,256]{2,1,0:T(8,128)S(1)} %fusion.23), channel_id=1, replica_groups=mesh['ctx'=16,'tis'=8,'rep'=4] {'tis'}, use_global_device_ids=true, to_apply=%region_10.12 | all-reduce | flops 4096 | bytes 32768 | tf_op jit(solution)/shard_map/psum | solution.py:110
  111.2 161.4 %all-reduce.4.cloned.1.call-done = f32[256,4,512]{2,0,1:T(8,128)} async-done(((f32[256,4,512]{2,0,1:T(8,128)}), f32[256,4,512]{2,0,1:T(8,128)}) %all-reduce.4.cloned.1.call-update) | async-done | bytes 2097168
  272.6 1.5 dynamic-slice_bitcast_fusion
  (65 shorter events, 3.7 us)
Async XLA Ops:
  7.2 20.0 %copy-start = (bf16[128,256]{1,0:T(8,128)(2,1)S(1)}, bf16[128,256]{1,0:T(8,128)(2,1)}, u32[]{:S(2)}) copy-start(bf16[128,256]{1,0:T(8,128)(2,1)} %param.17) | copy-start | bytes 196612
  7.2 265.4 %all-reduce.4.cloned.1.call-start = ((), (), s32[]{:S(2)}) async-start(), calls=%async_computation | async-start | bytes 4194304
  7.2 6.0 %collective-permute-start = (bf16[1,16,256]{2,1,0:T(8,128)(2,1)}, bf16[1,16,256]{2,1,0:T(8,128)(2,1)S(1)}, u32[]{:S(2)}, u32[]{:S(2)}) collective-permute-start(bf16[1,16,256]{2,1,0:T(8,128)(2,1)} %param.12), channel_id=1, source_target_pairs={{32,0},{64,32},{96,64},{128,96},{160,128},{192,160},{224,192},{256... | collective-permute-start | bytes 24584 | tf_op jit(solution)/shard_map/ppermute | solution.py:15
  13.2 3.7 %collective-permute-start.1 = (bf16[1,16,256]{2,1,0:T(8,128)(2,1)S(1)}, bf16[1,16,256]{2,1,0:T(8,128)(2,1)S(1)}, u32[]{:S(2)}, u32[]{:S(2)}) collective-permute-start(bf16[1,16,256]{2,1,0:T(8,128)(2,1)S(1)} %collective-permute-done), channel_id=1, source_target_pairs={{32,0},{64,32},{96,64},{128,96},{160,128},{192,160},{224,192},{256... | collective-permute-start | bytes 24584 | tf_op jit(solution)/shard_map/ppermute | solution.py:15
  16.9 5.2 %collective-permute-start.2 = (bf16[1,16,256]{2,1,0:T(8,128)(2,1)S(1)}, bf16[1,16,256]{2,1,0:T(8,128)(2,1)S(1)}, u32[]{:S(2)}, u32[]{:S(2)}) collective-permute-start(bf16[1,16,256]{2,1,0:T(8,128)(2,1)S(1)} %collective-permute-done.1), channel_id=1, source_target_pairs={{32,0},{64,32},{96,64},{128,96},{160,128},{192,160},{224,192},{256... | collective-permute-start | bytes 24584 | tf_op jit(solution)/shard_map/ppermute | solution.py:15
  22.2 5.0 %collective-permute-start.3 = (bf16[1,16,256]{2,1,0:T(8,128)(2,1)S(1)}, bf16[1,16,256]{2,1,0:T(8,128)(2,1)S(1)}, u32[]{:S(2)}, u32[]{:S(2)}) collective-permute-start(bf16[1,16,256]{2,1,0:T(8,128)(2,1)S(1)} %collective-permute-done.2), channel_id=1, source_target_pairs={{32,0},{64,32},{96,64},{128,96},{160,128},{192,160},{224,192},{256... | collective-permute-start | bytes 24584 | tf_op jit(solution)/shard_map/ppermute | solution.py:15
  27.1 1.7 copy-start.6
  34.3 2.3 copy-start.8
  37.1 1.7 copy-start.10
  37.2 1.7 copy-start.11
  55.5 1.3 copy-start.1
  55.5 1.6 copy-start.7
  58.3 1.3 copy-start.5
  58.9 5.6 %copy-start.2 = (f32[256,1,512]{2,0,1:T(8,128)S(1)}, f32[256,1,512]{2,0,1:T(8,128)}, u32[]{:S(2)}) copy-start(f32[256,1,512]{2,0,1:T(8,128)} %convolution_bitcast_fusion.3) | copy-start | bytes 1572868
  58.9 5.6 %copy-start.3 = (f32[256,1,512]{2,0,1:T(8,128)S(1)}, f32[256,1,512]{2,0,1:T(8,128)}, u32[]{:S(2)}) copy-start(f32[256,1,512]{2,0,1:T(8,128)} %convolution_bitcast_fusion) | copy-start | bytes 1572868
  58.9 5.6 %copy-start.4 = (f32[256,1,512]{2,0,1:T(8,128)S(1)}, f32[256,1,512]{2,0,1:T(8,128)}, u32[]{:S(2)}) copy-start(f32[256,1,512]{2,0,1:T(8,128)} %convolution_bitcast_fusion.1) | copy-start | bytes 1572868
  60.1 5.8 %collective-permute-start.4 = (f32[1,16,256]{2,1,0:T(8,128)S(1)}, f32[1,16,256]{2,1,0:T(8,128)S(1)}, u32[]{:S(2)}, u32[]{:S(2)}) collective-permute-start(f32[1,16,256]{2,1,0:T(8,128)S(1)} %slice_bitcast_fusion.4), channel_id=1, source_target_pairs={{0,32},{32,64},{64,96},{96,128},{128,160},{160,192},{192,224},{224... | collective-permute-start | bytes 49160 | tf_op jit(solution)/shard_map/ppermute | solution.py:15
  66.0 11.0 %copy-start.9 = (s32[1,16,4]{1,2,0:T(4,128)S(1)}, s32[1,16,4]{1,2,0:T(4,128)}, u32[]{:S(2)}) copy-start(s32[1,16,4]{1,2,0:T(4,128)} %param.16) | copy-start | bytes 772
  66.0 6.6 %collective-permute-start.5 = (f32[1,16,256]{2,1,0:T(8,128)S(1)}, f32[1,16,256]{2,1,0:T(8,128)S(1)}, u32[]{:S(2)}, u32[]{:S(2)}) collective-permute-start(f32[1,16,256]{2,1,0:T(8,128)S(1)} %fusion.26), channel_id=1, source_target_pairs={{0,32},{32,64},{64,96},{96,128},{128,160},{160,192},{192,224},{224... | collective-permute-start | bytes 49160 | tf_op jit(solution)/shard_map/ppermute | solution.py:15
  72.6 5.1 %collective-permute-start.6 = (f32[1,16,256]{2,1,0:T(8,128)S(1)}, f32[1,16,256]{2,1,0:T(8,128)S(1)}, u32[]{:S(2)}, u32[]{:S(2)}) collective-permute-start(f32[1,16,256]{2,1,0:T(8,128)S(1)} %fusion.25), channel_id=1, source_target_pairs={{0,32},{32,64},{64,96},{96,128},{128,160},{160,192},{192,224},{224... | collective-permute-start | bytes 49160 | tf_op jit(solution)/shard_map/ppermute | solution.py:15
  77.8 3.1 %collective-permute-start.7 = (f32[1,16,256]{2,1,0:T(8,128)S(1)}, f32[1,16,256]{2,1,0:T(8,128)S(1)}, u32[]{:S(2)}, u32[]{:S(2)}) collective-permute-start(f32[1,16,256]{2,1,0:T(8,128)S(1)} %fusion.24), channel_id=1, source_target_pairs={{0,32},{32,64},{64,96},{96,128},{128,160},{160,192},{192,224},{224... | collective-permute-start | bytes 49160 | tf_op jit(solution)/shard_map/ppermute | solution.py:15
Sparse Core Ops, SparseCore 0:
  66.1 206.4 all-reduce.3
where the time goes:
time: 282 us; the launch traced here: 281 us
  waiting for transfers between devices  172 us (61%)
  blocking collectives  30.4 us (11%)
  matrix products  20.5 us (7%)
  starting transfers between devices  18 us (6%)
  other arithmetic  15.4 us (5%)
  between operations  15.1 us (5%)
  local copies, waits for them, and re-layouts  9.11 us (3%)
    unnamed x2, waiting for transfers between devices  161 us
    psum x1, blocking collectives, on_device(): grad_acceptor = lax.psum(carried, 'tis')  30.4 us
    ppermute x8, starting transfers between devices, passed_along(): lax.ppermute(value, axis, [(source, source + steps) for source in range(f...  18 us
    ppermute x8, waiting for transfers between devices, passed_along(): lax.ppermute(value, axis, [(source, source + steps) for source in range(f...  11 us
    convert_element_type x4, other arithmetic, on_device(): grad_hid = (grad_act * silu_grad(hid)).astype(jnp.bfloat16)  9.15 us
    dot_general x4, matrix products, on_device(): hid = jnp.dot(flat, w_in, preferred_element_type=jnp.float32)  7.74 us
  transfers between devices with their start and end apart: 9, of which 6 were waited for; matrix products, arithmetic and copies ran while one was open for 4% of the time, Pallas kernels for 0%

commit v1 on v0

--- a/solution.py
+++ b/solution.py
@@ -107,7 +107,7 @@
     carried = contrib[:, reach - 1]
     for offset in range(reach - 2, -1, -1):
         carried = passed_along(carried, "ctx", 1) + contrib[:, offset]
-    grad_acceptor = lax.psum(carried, "tis")
+    grad_acceptor = jnp.sum(lax.all_gather(carried, "tis"), axis=0)
     donor_loss = jnp.stack(losses, axis=-1)
     return (donor_loss, grad_hidden, grad_acceptor)
 

time: 282 us -> 292 us (1.035)
  waiting for transfers between devices: 172 us -> 184 us
  blocking collectives: 30.4 us -> 26.8 us
    psum x1 -> x0, blocking collectives: 30.4 us -> none  [on_device(): grad_acceptor = lax.psum(carried, 'tis')]
    all_gather x0 -> x1, blocking collectives: none -> 26.8 us  [on_device(): grad_acceptor = jnp.sum(lax.all_gather(carried, 'tis'), axis=0)]
    unnamed x2, waiting for transfers between devices: 161 us -> 172 us
  transfers between devices with their start and end apart: 9 -> 9, of which waited for: 6 -> 7; matrix products, arithmetic and copies ran while one was open for 4% -> 4% of each run, Pallas kernels for 0% -> 0%
where the time goes in v1:
time: 292 us; the launch traced here: 291 us
  waiting for transfers between devices  184 us (63%)
  blocking collectives  26.8 us (9%)
  matrix products  19.8 us (7%)
  starting transfers between devices  18 us (6%)
  other arithmetic  17.9 us (6%)
  between operations  15.1 us (5%)
  local copies, waits for them, and re-layouts  9.92 us (3%)
    unnamed x2, waiting for transfers between devices  172 us
    all_gather x1, blocking collectives, on_device(): grad_acceptor = jnp.sum(lax.all_gather(carried, 'tis'), axis=0)  26.8 us
    ppermute x8, starting transfers between devices, passed_along(): lax.ppermute(value, axis, [(source, source + steps) for source in range(f...  18 us
    ppermute x8, waiting for transfers between devices, passed_along(): lax.ppermute(value, axis, [(source, source + steps) for source in range(f...  11.3 us
    convert_element_type x4, other arithmetic, on_device(): grad_hid = (grad_act * silu_grad(hid)).astype(jnp.bfloat16)  11 us
    dot_general x4, matrix products, on_device(): hid = jnp.dot(flat, w_in, preferred_element_type=jnp.float32)  9.21 us
  transfers between devices with their start and end apart: 9, of which 7 were waited for; matrix products, arithmetic and copies ran while one was open for 4% of the time, Pallas kernels for 0%

profile of v1, /device:TPU:8, one launch (start us, length us, event | category | flops | bytes accessed | tf_op | source)
XLA Modules:
  0.0 291.2 jit_solution(10986963086269245836)
XLA Ops:
  7.2 1.3 collective-permute-start
  8.5 0.7 constant_dynamic-update-slice_fusion.4
  9.2 0.7 bitcast_convert_fusion.1
  9.9 0.8 slice_bitcast_fusion.8
  10.8 0.9 slice_reduce_fusion.3
  11.6 0.8 bitcast_add_fusion.4
  12.4 0.7 fusion.28
  13.3 1.3 dynamic-slice
  15.2 1.3 collective-permute-start.1
  16.5 2.4 collective-permute-done.1
  18.9 1.3 collective-permute-start.2
  20.2 3.9 %collective-permute-done.2 = bf16[1,16,256]{2,1,0:T(8,128)(2,1)S(1)} collective-permute-done((bf16[1,16,256]{2,1,0:T(8,128)(2,1)S(1)}, bf16[1,16,256]{2,1,0:T(8,128)(2,1)S(1)}, u32[]{:S(2)}, u32[]{:S(2)}) %collective-permute-start.2) | collective-permute-done | bytes 8224 | tf_op jit(solution)/shard_map/ppermute | solution.py:15
  24.1 1.3 collective-permute-start.3
  25.4 3.7 %collective-permute-done.3 = bf16[1,16,256]{2,1,0:T(8,128)(2,1)S(1)} collective-permute-done((bf16[1,16,256]{2,1,0:T(8,128)(2,1)S(1)}, bf16[1,16,256]{2,1,0:T(8,128)(2,1)S(1)}, u32[]{:S(2)}, u32[]{:S(2)}) %collective-permute-start.3) | collective-permute-done | bytes 8224 | tf_op jit(solution)/shard_map/ppermute | solution.py:15
  29.1 1.6 multiply_convert_fusion.8
  30.7 2.3 multiply_convert_fusion.7
  33.0 2.3 multiply_convert_fusion.4
  35.3 2.3 multiply_convert_fusion.5
  37.6 2.3 multiply_convert_fusion.6
  40.5 0.6 fusion.42
  41.0 0.6 fusion.44
  41.6 0.6 fusion.46
  42.9 2.7 multiply_convert_fusion
  45.6 1.3 convolution_bitcast_fusion
  47.0 2.7 multiply_convert_fusion.1
  49.7 1.4 convolution_bitcast_fusion.1
  51.2 2.7 multiply_convert_fusion.2
  53.9 1.1 copy-done.1
  55.0 1.4 convolution_bitcast_fusion.2
  56.5 2.8 multiply_convert_fusion.3
  59.9 0.8 copy-done.2
  61.7 0.5 convolution_add_fusion
  62.3 0.8 copy-done.6
  63.5 4.3 %collective-permute-start.4 = (f32[1,16,256]{2,1,0:T(8,128)S(1)}, f32[1,16,256]{2,1,0:T(8,128)S(1)}, u32[]{:S(2)}, u32[]{:S(2)}) collective-permute-start(f32[1,16,256]{2,1,0:T(8,128)S(1)} %slice_bitcast_fusion.4), channel_id=1, source_target_pairs={{0,32},{32,64},{64,96},{96,128},{128,160},{160,192},{192,224},{224... | collective-permute-start | bytes 49160 | tf_op jit(solution)/shard_map/ppermute | solution.py:15
  68.7 2.2 collective-permute-start.5
  71.0 1.5 pad_maximum_fusion
  72.5 0.7 gather_fusion
  73.1 0.7 gather_fusion.1
  73.8 0.7 gather_fusion.3
  74.4 0.7 gather_fusion.2
  75.1 4.0 %collective-permute-start.6 = (f32[1,16,256]{2,1,0:T(8,128)S(1)}, f32[1,16,256]{2,1,0:T(8,128)S(1)}, u32[]{:S(2)}, u32[]{:S(2)}) collective-permute-start(f32[1,16,256]{2,1,0:T(8,128)S(1)} %fusion.25), channel_id=1, source_target_pairs={{0,32},{32,64},{64,96},{96,128},{128,160},{160,192},{192,224},{224... | collective-permute-start | bytes 49160 | tf_op jit(solution)/shard_map/ppermute | solution.py:15
  79.2 0.8 collective-permute-done.6
  80.0 2.3 collective-permute-start.7
  82.3 0.6 pad_maximum_fusion.1
  83.1 26.8 %all-gather = f32[8,16,256]{2,1,0:T(8,128)S(1)} all-gather(f32[1,16,256]{2,1,0:T(8,128)S(1)} %fusion.23), channel_id=2, replica_groups=mesh['ctx'=16,'tis'=8,'rep'=4] {'tis'}, dimensions={0}, use_global_device_ids=true | all-gather | bytes 147456 | tf_op jit(solution)/shard_map/all_gather | solution.py:110
  109.9 0.6 reduce.11
  110.5 172.4 %all-reduce.4.cloned.1.call-done = f32[256,4,512]{2,0,1:T(8,128)} async-done(((f32[256,4,512]{2,0,1:T(8,128)}), f32[256,4,512]{2,0,1:T(8,128)}) %all-reduce.4.cloned.1.call-update) | async-done | bytes 2097168
  282.9 1.5 dynamic-slice_bitcast_fusion
  (68 shorter events, 4.8 us)
Async XLA Ops:
  7.2 21.9 %copy-start = (bf16[128,256]{1,0:T(8,128)(2,1)S(1)}, bf16[128,256]{1,0:T(8,128)(2,1)}, u32[]{:S(2)}) copy-start(bf16[128,256]{1,0:T(8,128)(2,1)} %param.17) | copy-start | bytes 196612
  7.2 275.7 %all-reduce.4.cloned.1.call-start = ((), (), s32[]{:S(2)}) async-start(), calls=%async_computation | async-start | bytes 4194304
  7.2 8.0 %collective-permute-start = (bf16[1,16,256]{2,1,0:T(8,128)(2,1)}, bf16[1,16,256]{2,1,0:T(8,128)(2,1)S(1)}, u32[]{:S(2)}, u32[]{:S(2)}) collective-permute-start(bf16[1,16,256]{2,1,0:T(8,128)(2,1)} %param.12), channel_id=1, source_target_pairs={{32,0},{64,32},{96,64},{128,96},{160,128},{192,160},{224,192},{256... | collective-permute-start | bytes 24584 | tf_op jit(solution)/shard_map/ppermute | solution.py:15
  15.2 3.7 %collective-permute-start.1 = (bf16[1,16,256]{2,1,0:T(8,128)(2,1)S(1)}, bf16[1,16,256]{2,1,0:T(8,128)(2,1)S(1)}, u32[]{:S(2)}, u32[]{:S(2)}) collective-permute-start(bf16[1,16,256]{2,1,0:T(8,128)(2,1)S(1)} %collective-permute-done), channel_id=1, source_target_pairs={{32,0},{64,32},{96,64},{128,96},{160,128},{192,160},{224,192},{256... | collective-permute-start | bytes 24584 | tf_op jit(solution)/shard_map/ppermute | solution.py:15
  18.9 5.2 %collective-permute-start.2 = (bf16[1,16,256]{2,1,0:T(8,128)(2,1)S(1)}, bf16[1,16,256]{2,1,0:T(8,128)(2,1)S(1)}, u32[]{:S(2)}, u32[]{:S(2)}) collective-permute-start(bf16[1,16,256]{2,1,0:T(8,128)(2,1)S(1)} %collective-permute-done.1), channel_id=1, source_target_pairs={{32,0},{64,32},{96,64},{128,96},{160,128},{192,160},{224,192},{256... | collective-permute-start | bytes 24584 | tf_op jit(solution)/shard_map/ppermute | solution.py:15
  24.1 5.0 %collective-permute-start.3 = (bf16[1,16,256]{2,1,0:T(8,128)(2,1)S(1)}, bf16[1,16,256]{2,1,0:T(8,128)(2,1)S(1)}, u32[]{:S(2)}, u32[]{:S(2)}) collective-permute-start(bf16[1,16,256]{2,1,0:T(8,128)(2,1)S(1)} %collective-permute-done.2), channel_id=1, source_target_pairs={{32,0},{64,32},{96,64},{128,96},{160,128},{192,160},{224,192},{256... | collective-permute-start | bytes 24584 | tf_op jit(solution)/shard_map/ppermute | solution.py:15
  29.1 1.6 copy-start.7
  37.6 2.3 copy-start.9
  40.5 1.7 copy-start.11
  40.5 1.7 copy-start.12
  53.9 1.1 copy-start.1
  56.5 2.8 copy-start.8
  59.3 1.3 copy-start.2
  61.7 1.3 copy-start.6
  63.0 7.9 %copy-start.3 = (f32[256,1,512]{2,0,1:T(8,128)S(1)}, f32[256,1,512]{2,0,1:T(8,128)}, u32[]{:S(2)}) copy-start(f32[256,1,512]{2,0,1:T(8,128)} %convolution_bitcast_fusion) | copy-start | bytes 1572868
  63.0 7.9 %copy-start.4 = (f32[256,1,512]{2,0,1:T(8,128)S(1)}, f32[256,1,512]{2,0,1:T(8,128)}, u32[]{:S(2)}) copy-start(f32[256,1,512]{2,0,1:T(8,128)} %convolution_bitcast_fusion.1) | copy-start | bytes 1572868
  63.0 7.9 %copy-start.5 = (f32[256,1,512]{2,0,1:T(8,128)S(1)}, f32[256,1,512]{2,0,1:T(8,128)}, u32[]{:S(2)}) copy-start(f32[256,1,512]{2,0,1:T(8,128)} %convolution_bitcast_fusion.2) | copy-start | bytes 1572868
  63.5 5.2 %collective-permute-start.4 = (f32[1,16,256]{2,1,0:T(8,128)S(1)}, f32[1,16,256]{2,1,0:T(8,128)S(1)}, u32[]{:S(2)}, u32[]{:S(2)}) collective-permute-start(f32[1,16,256]{2,1,0:T(8,128)S(1)} %slice_bitcast_fusion.4), channel_id=1, source_target_pairs={{0,32},{32,64},{64,96},{96,128},{128,160},{160,192},{192,224},{224... | collective-permute-start | bytes 49160 | tf_op jit(solution)/shard_map/ppermute | solution.py:15
  68.7 6.4 %collective-permute-start.5 = (f32[1,16,256]{2,1,0:T(8,128)S(1)}, f32[1,16,256]{2,1,0:T(8,128)S(1)}, u32[]{:S(2)}, u32[]{:S(2)}) collective-permute-start(f32[1,16,256]{2,1,0:T(8,128)S(1)} %fusion.26), channel_id=1, source_target_pairs={{0,32},{32,64},{64,96},{96,128},{128,160},{160,192},{192,224},{224... | collective-permute-start | bytes 49160 | tf_op jit(solution)/shard_map/ppermute | solution.py:15
  72.4 6.7 %copy-start.10 = (s32[1,16,4]{1,2,0:T(4,128)S(1)}, s32[1,16,4]{1,2,0:T(4,128)}, u32[]{:S(2)}) copy-start(s32[1,16,4]{1,2,0:T(4,128)} %param.16) | copy-start | bytes 772
  75.1 4.9 %collective-permute-start.6 = (f32[1,16,256]{2,1,0:T(8,128)S(1)}, f32[1,16,256]{2,1,0:T(8,128)S(1)}, u32[]{:S(2)}, u32[]{:S(2)}) collective-permute-start(f32[1,16,256]{2,1,0:T(8,128)S(1)} %fusion.25), channel_id=1, source_target_pairs={{0,32},{32,64},{64,96},{96,128},{128,160},{160,192},{192,224},{224... | collective-permute-start | bytes 49160 | tf_op jit(solution)/shard_map/ppermute | solution.py:15
  80.0 3.1 %collective-permute-start.7 = (f32[1,16,256]{2,1,0:T(8,128)S(1)}, f32[1,16,256]{2,1,0:T(8,128)S(1)}, u32[]{:S(2)}, u32[]{:S(2)}) collective-permute-start(f32[1,16,256]{2,1,0:T(8,128)S(1)} %fusion.24), channel_id=1, source_target_pairs={{0,32},{32,64},{64,96},{96,128},{128,160},{160,192},{192,224},{224... | collective-permute-start | bytes 49160 | tf_op jit(solution)/shard_map/ppermute | solution.py:15
Sparse Core Ops, SparseCore 0:
  72.6 210.2 all-reduce.3
